TPU v7x, 32 devices: a whole 2x2x4 slice. The times are simulated.
32 devices in a mesh: gx: 8 (over y, x, core), gy: 4 (over z).
Axes of the slice: x: 2, y: 2, z: 4, core: 2. Of those that a mesh axis runs over, the one named last changes fastest.
Arguments:
- particle_count: int32 [8, 256, 1024], P(None, ('gx', 'gy')), may hold values from 0 to 12
- drag_coeff: float32 [8, 256, 1024], P(None, ('gx', 'gy')), may hold values from 0.05 to 2
- particle_velocity: float32 [3, 8, 256, 1024], P(None, None, ('gx', 'gy')), may hold values from -6 to 6
- fluid_velocity: float32 [3, 8, 256, 1024], P(None, None, 'gy', 'gx'), may hold values from -6 to 6
Outputs:
- pressure: float32 [8, 256, 1024], P(None, 'gy', 'gx')
- new_velocity: float32 [3, 8, 256, 1024], P(None, None, ('gx', 'gy'))
- pressure_gradient: float32 [3, 8, 256, 1024], P(None, None, ('gx', 'gy'))
All inputs are finite; a program needn't handle non-finite values.
Results may differ from a plain program's by a relative error of at most 0.00002.
Values sent between devices are 32-bit elements; how exact they have to be, the bound alone decides.
A program may use at most 64 MiB of HBM per device.

v0:
```python
import jax
import jax.numpy as jnp
from jax import lax
from jax.sharding import PartitionSpec as P

SWEEPS = 8
particle_volume = 0.05
time_step = 0.5
viscosity = 0.1


def padded_2(cells, sides, width):
    for axis, dim in sides:
        count = lax.axis_size(axis)
        ends = count - 1
        head = lax.slice_in_dim(cells, 0, width, axis=dim)
        tail = lax.slice_in_dim(cells, cells.shape[dim] - width, cells.shape[dim], axis=dim)
        cells = jnp.concatenate(
            [
                lax.ppermute(tail, axis, [(i, (i + 1) % count) for i in range(ends)]),
                cells,
                lax.ppermute(head, axis, [((i + 1) % count, i) for i in range(ends)]),
            ],
            axis=dim,
        )
    return cells


def pad_depth(values):
    widths = [(0, 0)] * (values.ndim - 3) + [(1, 1), (0, 0), (0, 0)]
    return jnp.pad(values, widths)


def pad_plane(values):
    widths = [(0, 0)] * (values.ndim - 2) + [(1, 1), (1, 1)]
    return jnp.pad(values, widths)


def pad_second(values):
    widths = [(0, 0)] * (values.ndim - 1) + [(1, 1)]
    return jnp.pad(values, widths)


def middle(values):
    return values[..., 1:-1, 1:-1, 1:-1]


def neighbour(values, which):
    if which == 0:
        return values[..., 2:, 1:-1, 1:-1]
    if which == 1:
        return values[..., :-2, 1:-1, 1:-1]
    if which == 2:
        return values[..., 1:-1, 2:, 1:-1]
    if which == 3:
        return values[..., 1:-1, :-2, 1:-1]
    if which == 4:
        return values[..., 1:-1, 1:-1, 2:]
    return values[..., 1:-1, 1:-1, :-2]


def face_weights(voids_wide):
    padded = pad_depth(voids_wide)
    centre = middle(padded)
    weights = jnp.stack([0.5 * (centre + neighbour(padded, which)) for which in range(6)])
    weight_sum = weights[0]
    for which in range(1, 6):
        weight_sum = weight_sum + weights[which]
    return (weights, weight_sum)


def momentum(velocity_wide, weights, voids, drag, drag_force):
    padded = pad_depth(velocity_wide)
    centre = middle(padded)
    diffusion = jnp.zeros_like(centre)
    for which in range(6):
        diffusion = diffusion + weights[which][None] * (neighbour(padded, which) - centre)
    return (voids[None] * centre + time_step * viscosity * diffusion + time_step * drag_force) / (
        voids[None] + time_step * drag[None]
    )


def divergence(flux_wide):
    first = flux_wide[0][:, 2:, 1:-1] - flux_wide[0][:, :-2, 1:-1]
    second = flux_wide[1][:, 1:-1, 2:] - flux_wide[1][:, 1:-1, :-2]
    normal = pad_depth(flux_wide[2])[:, 1:-1, 1:-1]
    third = normal[2:] - normal[:-2]
    return 0.5 * (first + second + third) / time_step


def jacobi_sweep(pressure_wide, weights, weight_sum, source):
    padded = pad_depth(pressure_wide)
    total = weights[0] * neighbour(padded, 0)
    for which in range(1, 6):
        total = total + weights[which] * neighbour(padded, which)
    return (total - source) / weight_sum


def gradient_of(pressure_wide):
    padded = pad_depth(pressure_wide)
    first = 0.5 * (padded[1:-1, 2:, 1:-1] - padded[1:-1, :-2, 1:-1])
    second = 0.5 * (padded[1:-1, 1:-1, 2:] - padded[1:-1, 1:-1, :-2])
    third = 0.5 * (padded[2:, 1:-1, 1:-1] - padded[:-2, 1:-1, 1:-1])
    return jnp.stack([first, second, third])


def order_inward(values, across, along):
    fields, planes, x_rows, y_cols = values.shape
    groups = across // along
    rows_each = x_rows // across
    shaped = values.reshape(fields, planes, along, groups, rows_each, y_cols)
    return jnp.swapaxes(shaped, 2, 3).reshape(fields, planes, x_rows, y_cols)


def order_outward(values, across, along):
    fields, planes, x_rows, y_cols = values.shape
    groups = across // along
    rows_each = x_rows // across
    shaped = values.reshape(fields, planes, groups, along, rows_each, y_cols)
    return jnp.swapaxes(shaped, 2, 3).reshape(fields, planes, x_rows, y_cols)


def to_fluid(fields):
    moved = lax.all_to_all(
        lax.all_to_all(fields, "gx", split_axis=3, concat_axis=2, tiled=True),
        "gy",
        split_axis=2,
        concat_axis=2,
        tiled=True,
    )
    return order_inward(moved, lax.axis_size("gx"), lax.axis_size("gy"))


def to_particles(fields):
    ordered = order_outward(fields, lax.axis_size("gx"), lax.axis_size("gy"))
    return lax.all_to_all(
        lax.all_to_all(ordered, "gy", split_axis=2, concat_axis=2, tiled=True),
        "gx",
        split_axis=2,
        concat_axis=3,
        tiled=True,
    )


def shards(particle_count, drag_coeff, particle_velocity, fluid_velocity):
    voids = 1.0 - particle_count.astype(jnp.float32) * particle_volume
    drag_force = drag_coeff[None] * particle_velocity
    slab_velocity = to_particles(fluid_velocity)
    stacked = jnp.concatenate([slab_velocity, voids[None]], axis=0)
    widened = pad_second(padded_2(stacked, ((("gx", "gy"), 2),), 1))
    weights, weight_sum = face_weights(widened[3])
    predicted = momentum(widened[:3], weights, voids, drag_coeff, drag_force)
    flux = voids[None] * predicted
    flux_first = pad_second(padded_2(flux[0:1], ((("gx", "gy"), 2),), 1))
    flux_wide = jnp.concatenate([flux_first, pad_plane(flux[1:3])], axis=0)
    source = divergence(flux_wide)
    pressure = -source / weight_sum
    for sweep_index in range(SWEEPS - 1):
        pressure_wide = pad_second(padded_2(pressure, ((("gx", "gy"), 1),), 1))
        pressure = jacobi_sweep(pressure_wide, weights, weight_sum, source)
    final_wide = pad_second(padded_2(pressure, ((("gx", "gy"), 1),), 1))
    slopes = gradient_of(final_wide)
    velocity = predicted - time_step * slopes
    pressure_out = to_fluid(pressure[None])[0]
    return (pressure_out, velocity, slopes)


def solution(mesh):
    placed = (
        P(None, ("gx", "gy"), None),
        P(None, ("gx", "gy"), None),
        P(None, None, ("gx", "gy"), None),
        P(None, None, "gy", "gx"),
    )
    return jax.shard_map(
        shards,
        mesh=mesh,
        in_specs=placed,
        out_specs=(
            P(None, "gy", "gx"),
            P(None, None, ("gx", "gy"), None),
            P(None, None, ("gx", "gy"), None),
        ),
        check_vma=False,
    )
```

profile of v0, /device:TPU:0, one launch (start us, length us, event | category | flops | bytes accessed | tf_op | source)
XLA Modules:
  0.0 200.9 jit_solution(16246067221753685963)
XLA Ops:
  2.3 26.5 %all_to_all.46 = f32[3,8,64,128]{3,1,0,2:T(8,128)} all-to-all(f32[3,8,64,128]{3,1,0,2:T(8,128)S(1)} %copy.52), channel_id=1, replica_groups=mesh['gx'=8,'gy'=4] {'gy'}, dimensions={2} | all-to-all | bytes 1572864 | tf_op jit(solution)/shard_map/all_to_all | solution.py:137
  28.8 3.7 %all-to-all-start.1 = ((f32[3,8,64,128]{3,1,0,2:T(8,128)}), f32[3,8,64,128]{3,1,0,2:T(8,128)S(1)}, u32[]{:S(2)}, u32[]{:S(2)}) async-start(f32[3,8,64,128]{3,1,0,2:T(8,128)} %all_to_all.46), calls=%async_computation.1 | async-start | bytes 1572864 | tf_op jit(solution)/shard_map/all_to_all | solution.py:136
  32.9 12.2 %all-to-all-done.1 = f32[3,8,64,128]{3,1,0,2:T(8,128)S(1)} async-done(((f32[3,8,64,128]{3,1,0,2:T(8,128)}), f32[3,8,64,128]{3,1,0,2:T(8,128)S(1)}, u32[]{:S(2)}, u32[]{:S(2)}) %all-to-all-start.1) | async-done | bytes 786464 | tf_op jit(solution)/shard_map/all_to_all | solution.py:136
  49.8 4.8 %collective-permute-done.1 = f32[4,8,1,1024]{3,1,2,0:T(8,128)S(1)} collective-permute-done((f32[4,8,1,1024]{3,1,2,0:T(8,128)S(1)}, f32[4,8,1,1024]{3,1,2,0:T(8,128)S(1)}, u32[]{:S(2)}, u32[]{:S(2)}) %collective-permute-start.1) | collective-permute-done | bytes 131104 | tf_op jit(solution)/shard_map/ppermute | solution.py:22
  61.9 4.7 %collective-permute-done.3 = f32[1,8,1,1024]{3,1,2,0:T(8,128)S(1)} collective-permute-done((f32[1,8,1,1024]{3,1,2,0:T(8,128)S(1)}, f32[1,8,1,1024]{3,1,2,0:T(8,128)S(1)}, u32[]{:S(2)}, u32[]{:S(2)}) %collective-permute-start.3) | collective-permute-done | bytes 32800 | tf_op jit(solution)/shard_map/ppermute | solution.py:22
  67.2 3.9 %collective-permute-start.4 = (f32[8,1,1024]{2,0,1:T(8,128)S(1)}, f32[8,1,1024]{2,0,1:T(8,128)S(1)}, u32[]{:S(2)}, u32[]{:S(2)}) collective-permute-start(f32[8,1,1024]{2,0,1:T(8,128)S(1)} %get-tuple-element.46), channel_id=1, source_target_pairs={{0,1},{1,2},{2,3},{3,4},{4,5},{5,6},{6,7},{7,8},{8,9},{9,10},{10,1... | collective-permute-start | bytes 98312 | tf_op jit(solution)/shard_map/ppermute | solution.py:20
  72.7 4.2 %collective-permute-done.5 = f32[8,1,1024]{2,0,1:T(8,128)S(1)} collective-permute-done((f32[8,1,1024]{2,0,1:T(8,128)S(1)}, f32[8,1,1024]{2,0,1:T(8,128)S(1)}, u32[]{:S(2)}, u32[]{:S(2)}) %collective-permute-start.5) | collective-permute-done | bytes 32800 | tf_op jit(solution)/shard_map/ppermute | solution.py:22
  81.4 4.2 %collective-permute-done.7 = f32[8,1,1024]{2,0,1:T(8,128)S(1)} collective-permute-done((f32[8,1,1024]{2,0,1:T(8,128)S(1)}, f32[8,1,1024]{2,0,1:T(8,128)S(1)}, u32[]{:S(2)}, u32[]{:S(2)}) %collective-permute-start.7) | collective-permute-done | bytes 32800 | tf_op jit(solution)/shard_map/ppermute | solution.py:22
  90.8 4.2 %collective-permute-done.9 = f32[8,1,1024]{2,0,1:T(8,128)S(1)} collective-permute-done((f32[8,1,1024]{2,0,1:T(8,128)S(1)}, f32[8,1,1024]{2,0,1:T(8,128)S(1)}, u32[]{:S(2)}, u32[]{:S(2)}) %collective-permute-start.9) | collective-permute-done | bytes 32800 | tf_op jit(solution)/shard_map/ppermute | solution.py:22
  95.6 4.1 %collective-permute-start.10 = (f32[8,1,1024]{2,0,1:T(8,128)S(1)}, f32[8,1,1024]{2,0,1:T(8,128)S(1)}, u32[]{:S(2)}, u32[]{:S(2)}) collective-permute-start(f32[8,1,1024]{2,0,1:T(8,128)S(1)} %get-tuple-element.40), channel_id=1, source_target_pairs={{0,1},{1,2},{2,3},{3,4},{4,5},{5,6},{6,7},{7,8},{8,9},{9,10},{10,1... | collective-permute-start | bytes 98312 | tf_op jit(solution)/shard_map/ppermute | solution.py:20
  101.3 4.6 %collective-permute-done.11 = f32[8,1,1024]{2,0,1:T(8,128)S(1)} collective-permute-done((f32[8,1,1024]{2,0,1:T(8,128)S(1)}, f32[8,1,1024]{2,0,1:T(8,128)S(1)}, u32[]{:S(2)}, u32[]{:S(2)}) %collective-permute-start.11) | collective-permute-done | bytes 32800 | tf_op jit(solution)/shard_map/ppermute | solution.py:22
  106.5 3.9 %collective-permute-start.12 = (f32[8,1,1024]{2,0,1:T(8,128)S(1)}, f32[8,1,1024]{2,0,1:T(8,128)S(1)}, u32[]{:S(2)}, u32[]{:S(2)}) collective-permute-start(f32[8,1,1024]{2,0,1:T(8,128)S(1)} %get-tuple-element.38), channel_id=1, source_target_pairs={{0,1},{1,2},{2,3},{3,4},{4,5},{5,6},{6,7},{7,8},{8,9},{9,10},{10,1... | collective-permute-start | bytes 98312 | tf_op jit(solution)/shard_map/ppermute | solution.py:20
  112.1 4.6 %collective-permute-done.13 = f32[8,1,1024]{2,0,1:T(8,128)S(1)} collective-permute-done((f32[8,1,1024]{2,0,1:T(8,128)S(1)}, f32[8,1,1024]{2,0,1:T(8,128)S(1)}, u32[]{:S(2)}, u32[]{:S(2)}) %collective-permute-start.13) | collective-permute-done | bytes 32800 | tf_op jit(solution)/shard_map/ppermute | solution.py:22
  117.3 3.7 %collective-permute-start.14 = (f32[8,1,1024]{2,0,1:T(8,128)S(1)}, f32[8,1,1024]{2,0,1:T(8,128)S(1)}, u32[]{:S(2)}, u32[]{:S(2)}) collective-permute-start(f32[8,1,1024]{2,0,1:T(8,128)S(1)} %get-tuple-element.36), channel_id=1, source_target_pairs={{0,1},{1,2},{2,3},{3,4},{4,5},{5,6},{6,7},{7,8},{8,9},{9,10},{10,1... | collective-permute-start | bytes 98312 | tf_op jit(solution)/shard_map/ppermute | solution.py:20
  122.6 4.6 %collective-permute-done.15 = f32[8,1,1024]{2,0,1:T(8,128)S(1)} collective-permute-done((f32[8,1,1024]{2,0,1:T(8,128)S(1)}, f32[8,1,1024]{2,0,1:T(8,128)S(1)}, u32[]{:S(2)}, u32[]{:S(2)}) %collective-permute-start.15) | collective-permute-done | bytes 32800 | tf_op jit(solution)/shard_map/ppermute | solution.py:22
  127.7 3.7 %collective-permute-start.16 = (f32[8,1,1024]{2,0,1:T(8,128)S(1)}, f32[8,1,1024]{2,0,1:T(8,128)S(1)}, u32[]{:S(2)}, u32[]{:S(2)}) collective-permute-start(f32[8,1,1024]{2,0,1:T(8,128)S(1)} %get-tuple-element.34), channel_id=1, source_target_pairs={{0,1},{1,2},{2,3},{3,4},{4,5},{5,6},{6,7},{7,8},{8,9},{9,10},{10,1... | collective-permute-start | bytes 98312 | tf_op jit(solution)/shard_map/ppermute | solution.py:20
  133.0 4.6 %collective-permute-done.17 = f32[8,1,1024]{2,0,1:T(8,128)S(1)} collective-permute-done((f32[8,1,1024]{2,0,1:T(8,128)S(1)}, f32[8,1,1024]{2,0,1:T(8,128)S(1)}, u32[]{:S(2)}, u32[]{:S(2)}) %collective-permute-start.17) | collective-permute-done | bytes 32800 | tf_op jit(solution)/shard_map/ppermute | solution.py:22
  139.5 4.5 %collective-permute-start.19 = (f32[8,1,1024]{2,0,1:T(8,128)S(1)}, f32[8,1,1024]{2,0,1:T(8,128)S(1)}, u32[]{:S(2)}, u32[]{:S(2)}) collective-permute-start(f32[8,1,1024]{2,0,1:T(8,128)S(1)} %get-tuple-element.32), channel_id=1, source_target_pairs={{0,1},{1,2},{2,3},{3,4},{4,5},{5,6},{6,7},{7,8},{8,9},{9,10},{10,1... | collective-permute-start | bytes 98312 | tf_op jit(solution)/shard_map/ppermute | solution.py:20
  146.8 4.4 %reshape.29 = f32[8,1,8192]{2,1,0:T(1,128)} reshape(f32[1024,1,8,8]{3,2,1,0:T(8,128)} %bitcast.38) | data formatting | bytes 524288
  151.2 18.5 %all-to-all-start.2 = ((f32[8,1,8192]{2,1,0:T(1,128)}), f32[8,1,8192]{2,1,0:T(1,128)S(1)}, u32[]{:S(2)}, u32[]{:S(2)}) async-start(f32[8,1,8192]{2,1,0:T(1,128)} %reshape.29), calls=%async_computation.2 | async-start | bytes 524288 | tf_op jit(solution)/shard_map/all_to_all | solution.py:125
  169.8 6.7 %all-to-all-done.2 = f32[8,1,8192]{2,1,0:T(1,128)S(1)} async-done(((f32[8,1,8192]{2,1,0:T(1,128)}), f32[8,1,8192]{2,1,0:T(1,128)S(1)}, u32[]{:S(2)}, u32[]{:S(2)}) %all-to-all-start.2) | async-done | bytes 262176 | tf_op jit(solution)/shard_map/all_to_all | solution.py:125
  178.4 4.3 %reshape.30 = f32[1024,1,8,8]{3,2,1,0:T(8,128)} reshape(f32[8,8192]{1,0:T(8,128)S(1)} %reduce) | data formatting | bytes 524288
  186.1 5.7 %all-to-all-start.3 = ((f32[1,8,64,128]{3,1,0,2:T(8,128)}), f32[1,8,64,128]{3,1,0,2:T(8,128)S(1)}, u32[]{:S(2)}, u32[]{:S(2)}) async-start(f32[1,8,64,128]{3,1,0,2:T(8,128)} %bitcast.14), calls=%async_computation.3 | async-start | bytes 524288 | tf_op jit(solution)/shard_map/all_to_all | solution.py:124
  194.9 5.2 %all-to-all-done.3 = f32[1,8,64,128]{3,1,0,2:T(8,128)S(1)} async-done(((f32[1,8,64,128]{3,1,0,2:T(8,128)}), f32[1,8,64,128]{3,1,0,2:T(8,128)S(1)}, u32[]{:S(2)}, u32[]{:S(2)}) %all-to-all-start.3) | async-done | bytes 262176 | tf_op jit(solution)/shard_map/all_to_all | solution.py:124
  (80 shorter events, 48.2 us)
Async XLA Ops:
  2.3 30.2 %copy-start.1 = (f32[8,8,1024]{2,1,0:T(8,128)S(1)}, f32[8,8,1024]{2,1,0:T(8,128)}, u32[]{:S(2)}) copy-start(f32[8,8,1024]{2,1,0:T(8,128)} %param.5) | copy-start | bytes 786436
  28.8 16.3 %all-to-all-start.1 = ((f32[3,8,64,128]{3,1,0,2:T(8,128)}), f32[3,8,64,128]{3,1,0,2:T(8,128)S(1)}, u32[]{:S(2)}, u32[]{:S(2)}) async-start(f32[3,8,64,128]{3,1,0,2:T(8,128)} %all_to_all.46), calls=%async_computation.1 | async-start | bytes 1572864 | tf_op jit(solution)/shard_map/all_to_all | solution.py:136
  45.2 4.6 %collective-permute-start = (f32[4,8,1,1024]{3,1,2,0:T(8,128)S(1)}, f32[4,8,1,1024]{3,1,2,0:T(8,128)S(1)}, u32[]{:S(2)}, u32[]{:S(2)}) collective-permute-start(f32[4,8,1,1024]{3,1,2,0:T(8,128)S(1)} %get-tuple-element.16), channel_id=1, source_target_pairs={{0,1},{1,2},{2,3},{3,4},{4,5},{5,6},{6,7},{7,8},{8,9},{9,10},{10,1... | collective-permute-start | bytes 393224 | tf_op jit(solution)/shard_map/ppermute | solution.py:20
  47.3 7.3 %collective-permute-start.1 = (f32[4,8,1,1024]{3,1,2,0:T(8,128)S(1)}, f32[4,8,1,1024]{3,1,2,0:T(8,128)S(1)}, u32[]{:S(2)}, u32[]{:S(2)}) collective-permute-start(f32[4,8,1,1024]{3,1,2,0:T(8,128)S(1)} %get-tuple-element.17), channel_id=1, source_target_pairs={{1,0},{2,1},{3,2},{4,3},{5,4},{6,5},{7,6},{8,7},{9,8},{10,9},{11,1... | collective-permute-start | bytes 393224 | tf_op jit(solution)/shard_map/ppermute | solution.py:22
  57.8 4.1 %collective-permute-start.2 = (f32[1,8,1,1024]{3,1,2,0:T(8,128)S(1)}, f32[1,8,1,1024]{3,1,2,0:T(8,128)S(1)}, u32[]{:S(2)}, u32[]{:S(2)}) collective-permute-start(f32[1,8,1,1024]{3,1,2,0:T(8,128)S(1)} %get-tuple-element.20), channel_id=1, source_target_pairs={{0,1},{1,2},{2,3},{3,4},{4,5},{5,6},{6,7},{7,8},{8,9},{9,10},{10,1... | collective-permute-start | bytes 98312 | tf_op jit(solution)/shard_map/ppermute | solution.py:20
  60.3 6.3 %collective-permute-start.3 = (f32[1,8,1,1024]{3,1,2,0:T(8,128)S(1)}, f32[1,8,1,1024]{3,1,2,0:T(8,128)S(1)}, u32[]{:S(2)}, u32[]{:S(2)}) collective-permute-start(f32[1,8,1,1024]{3,1,2,0:T(8,128)S(1)} %get-tuple-element.21), channel_id=1, source_target_pairs={{1,0},{2,1},{3,2},{4,3},{5,4},{6,5},{7,6},{8,7},{9,8},{10,9},{11,1... | collective-permute-start | bytes 98312 | tf_op jit(solution)/shard_map/ppermute | solution.py:22
  67.2 5.5 %collective-permute-start.4 = (f32[8,1,1024]{2,0,1:T(8,128)S(1)}, f32[8,1,1024]{2,0,1:T(8,128)S(1)}, u32[]{:S(2)}, u32[]{:S(2)}) collective-permute-start(f32[8,1,1024]{2,0,1:T(8,128)S(1)} %get-tuple-element.46), channel_id=1, source_target_pairs={{0,1},{1,2},{2,3},{3,4},{4,5},{5,6},{6,7},{7,8},{8,9},{9,10},{10,1... | collective-permute-start | bytes 98312 | tf_op jit(solution)/shard_map/ppermute | solution.py:20
  71.2 5.8 %collective-permute-start.5 = (f32[8,1,1024]{2,0,1:T(8,128)S(1)}, f32[8,1,1024]{2,0,1:T(8,128)S(1)}, u32[]{:S(2)}, u32[]{:S(2)}) collective-permute-start(f32[8,1,1024]{2,0,1:T(8,128)S(1)} %get-tuple-element.47), channel_id=1, source_target_pairs={{1,0},{2,1},{3,2},{4,3},{5,4},{6,5},{7,6},{8,7},{9,8},{10,9},{11,1... | collective-permute-start | bytes 98312 | tf_op jit(solution)/shard_map/ppermute | solution.py:22
  77.6 3.8 %collective-permute-start.6 = (f32[8,1,1024]{2,0,1:T(8,128)S(1)}, f32[8,1,1024]{2,0,1:T(8,128)S(1)}, u32[]{:S(2)}, u32[]{:S(2)}) collective-permute-start(f32[8,1,1024]{2,0,1:T(8,128)S(1)} %get-tuple-element.44), channel_id=1, source_target_pairs={{0,1},{1,2},{2,3},{3,4},{4,5},{5,6},{6,7},{7,8},{8,9},{9,10},{10,1... | collective-permute-start | bytes 98312 | tf_op jit(solution)/shard_map/ppermute | solution.py:20
  79.8 5.8 %collective-permute-start.7 = (f32[8,1,1024]{2,0,1:T(8,128)S(1)}, f32[8,1,1024]{2,0,1:T(8,128)S(1)}, u32[]{:S(2)}, u32[]{:S(2)}) collective-permute-start(f32[8,1,1024]{2,0,1:T(8,128)S(1)} %get-tuple-element.45), channel_id=1, source_target_pairs={{1,0},{2,1},{3,2},{4,3},{5,4},{6,5},{7,6},{8,7},{9,8},{10,9},{11,1... | collective-permute-start | bytes 98312 | tf_op jit(solution)/shard_map/ppermute | solution.py:22
  86.3 4.5 %collective-permute-start.8 = (f32[8,1,1024]{2,0,1:T(8,128)S(1)}, f32[8,1,1024]{2,0,1:T(8,128)S(1)}, u32[]{:S(2)}, u32[]{:S(2)}) collective-permute-start(f32[8,1,1024]{2,0,1:T(8,128)S(1)} %get-tuple-element.42), channel_id=1, source_target_pairs={{0,1},{1,2},{2,3},{3,4},{4,5},{5,6},{6,7},{7,8},{8,9},{9,10},{10,1... | collective-permute-start | bytes 98312 | tf_op jit(solution)/shard_map/ppermute | solution.py:20
  89.2 5.8 %collective-permute-start.9 = (f32[8,1,1024]{2,0,1:T(8,128)S(1)}, f32[8,1,1024]{2,0,1:T(8,128)S(1)}, u32[]{:S(2)}, u32[]{:S(2)}) collective-permute-start(f32[8,1,1024]{2,0,1:T(8,128)S(1)} %get-tuple-element.43), channel_id=1, source_target_pairs={{1,0},{2,1},{3,2},{4,3},{5,4},{6,5},{7,6},{8,7},{9,8},{10,9},{11,1... | collective-permute-start | bytes 98312 | tf_op jit(solution)/shard_map/ppermute | solution.py:22
  95.6 5.7 %collective-permute-start.10 = (f32[8,1,1024]{2,0,1:T(8,128)S(1)}, f32[8,1,1024]{2,0,1:T(8,128)S(1)}, u32[]{:S(2)}, u32[]{:S(2)}) collective-permute-start(f32[8,1,1024]{2,0,1:T(8,128)S(1)} %get-tuple-element.40), channel_id=1, source_target_pairs={{0,1},{1,2},{2,3},{3,4},{4,5},{5,6},{6,7},{7,8},{8,9},{9,10},{10,1... | collective-permute-start | bytes 98312 | tf_op jit(solution)/shard_map/ppermute | solution.py:20
  99.7 6.2 %collective-permute-start.11 = (f32[8,1,1024]{2,0,1:T(8,128)S(1)}, f32[8,1,1024]{2,0,1:T(8,128)S(1)}, u32[]{:S(2)}, u32[]{:S(2)}) collective-permute-start(f32[8,1,1024]{2,0,1:T(8,128)S(1)} %get-tuple-element.41), channel_id=1, source_target_pairs={{1,0},{2,1},{3,2},{4,3},{5,4},{6,5},{7,6},{8,7},{9,8},{10,9},{11,1... | collective-permute-start | bytes 98312 | tf_op jit(solution)/shard_map/ppermute | solution.py:22
  106.5 5.5 %collective-permute-start.12 = (f32[8,1,1024]{2,0,1:T(8,128)S(1)}, f32[8,1,1024]{2,0,1:T(8,128)S(1)}, u32[]{:S(2)}, u32[]{:S(2)}) collective-permute-start(f32[8,1,1024]{2,0,1:T(8,128)S(1)} %get-tuple-element.38), channel_id=1, source_target_pairs={{0,1},{1,2},{2,3},{3,4},{4,5},{5,6},{6,7},{7,8},{8,9},{9,10},{10,1... | collective-permute-start | bytes 98312 | tf_op jit(solution)/shard_map/ppermute | solution.py:20
  110.5 6.1 %collective-permute-start.13 = (f32[8,1,1024]{2,0,1:T(8,128)S(1)}, f32[8,1,1024]{2,0,1:T(8,128)S(1)}, u32[]{:S(2)}, u32[]{:S(2)}) collective-permute-start(f32[8,1,1024]{2,0,1:T(8,128)S(1)} %get-tuple-element.39), channel_id=1, source_target_pairs={{1,0},{2,1},{3,2},{4,3},{5,4},{6,5},{7,6},{8,7},{9,8},{10,9},{11,1... | collective-permute-start | bytes 98312 | tf_op jit(solution)/shard_map/ppermute | solution.py:22
  117.3 5.3 %collective-permute-start.14 = (f32[8,1,1024]{2,0,1:T(8,128)S(1)}, f32[8,1,1024]{2,0,1:T(8,128)S(1)}, u32[]{:S(2)}, u32[]{:S(2)}) collective-permute-start(f32[8,1,1024]{2,0,1:T(8,128)S(1)} %get-tuple-element.36), channel_id=1, source_target_pairs={{0,1},{1,2},{2,3},{3,4},{4,5},{5,6},{6,7},{7,8},{8,9},{9,10},{10,1... | collective-permute-start | bytes 98312 | tf_op jit(solution)/shard_map/ppermute | solution.py:20
  121.0 6.1 %collective-permute-start.15 = (f32[8,1,1024]{2,0,1:T(8,128)S(1)}, f32[8,1,1024]{2,0,1:T(8,128)S(1)}, u32[]{:S(2)}, u32[]{:S(2)}) collective-permute-start(f32[8,1,1024]{2,0,1:T(8,128)S(1)} %get-tuple-element.37), channel_id=1, source_target_pairs={{1,0},{2,1},{3,2},{4,3},{5,4},{6,5},{7,6},{8,7},{9,8},{10,9},{11,1... | collective-permute-start | bytes 98312 | tf_op jit(solution)/shard_map/ppermute | solution.py:22
  127.7 5.3 %collective-permute-start.16 = (f32[8,1,1024]{2,0,1:T(8,128)S(1)}, f32[8,1,1024]{2,0,1:T(8,128)S(1)}, u32[]{:S(2)}, u32[]{:S(2)}) collective-permute-start(f32[8,1,1024]{2,0,1:T(8,128)S(1)} %get-tuple-element.34), channel_id=1, source_target_pairs={{0,1},{1,2},{2,3},{3,4},{4,5},{5,6},{6,7},{7,8},{8,9},{9,10},{10,1... | collective-permute-start | bytes 98312 | tf_op jit(solution)/shard_map/ppermute | solution.py:20
  131.5 6.1 %collective-permute-start.17 = (f32[8,1,1024]{2,0,1:T(8,128)S(1)}, f32[8,1,1024]{2,0,1:T(8,128)S(1)}, u32[]{:S(2)}, u32[]{:S(2)}) collective-permute-start(f32[8,1,1024]{2,0,1:T(8,128)S(1)} %get-tuple-element.35), channel_id=1, source_target_pairs={{1,0},{2,1},{3,2},{4,3},{5,4},{6,5},{7,6},{8,7},{9,8},{10,9},{11,1... | collective-permute-start | bytes 98312 | tf_op jit(solution)/shard_map/ppermute | solution.py:22
  138.2 31.4 %collective-permute-start.18 = (f32[8,1,1024]{2,0,1:T(8,128)S(1)}, f32[8,1,1024]{2,0,1:T(8,128)S(1)}, u32[]{:S(2)}, u32[]{:S(2)}) collective-permute-start(f32[8,1,1024]{2,0,1:T(8,128)S(1)} %get-tuple-element.33), channel_id=1, source_target_pairs={{1,0},{2,1},{3,2},{4,3},{5,4},{6,5},{7,6},{8,7},{9,8},{10,9},{11,1... | collective-permute-start | bytes 98312 | tf_op jit(solution)/shard_map/ppermute | solution.py:22
  139.5 30.1 %collective-permute-start.19 = (f32[8,1,1024]{2,0,1:T(8,128)S(1)}, f32[8,1,1024]{2,0,1:T(8,128)S(1)}, u32[]{:S(2)}, u32[]{:S(2)}) collective-permute-start(f32[8,1,1024]{2,0,1:T(8,128)S(1)} %get-tuple-element.32), channel_id=1, source_target_pairs={{0,1},{1,2},{2,3},{3,4},{4,5},{5,6},{6,7},{7,8},{8,9},{9,10},{10,1... | collective-permute-start | bytes 98312 | tf_op jit(solution)/shard_map/ppermute | solution.py:20
  151.2 25.4 %all-to-all-start.2 = ((f32[8,1,8192]{2,1,0:T(1,128)}), f32[8,1,8192]{2,1,0:T(1,128)S(1)}, u32[]{:S(2)}, u32[]{:S(2)}) async-start(f32[8,1,8192]{2,1,0:T(1,128)} %reshape.29), calls=%async_computation.2 | async-start | bytes 524288 | tf_op jit(solution)/shard_map/all_to_all | solution.py:125
  186.1 14.0 %all-to-all-start.3 = ((f32[1,8,64,128]{3,1,0,2:T(8,128)}), f32[1,8,64,128]{3,1,0,2:T(8,128)S(1)}, u32[]{:S(2)}, u32[]{:S(2)}) async-start(f32[1,8,64,128]{3,1,0,2:T(8,128)} %bitcast.14), calls=%async_computation.3 | async-start | bytes 524288 | tf_op jit(solution)/shard_map/all_to_all | solution.py:124
  (2 other events, 31.4 us)
where the time goes:
time: 202 us; the launch traced here: 201 us
  starting transfers between devices  74.5 us (37%)
  waiting for transfers between devices  67.8 us (34%)
  blocking collectives  26.5 us (13%)
  local copies, waits for them, and re-layouts  21.6 us (11%)
  other arithmetic  9.39 us (5%)
    ppermute x10, waiting for transfers between devices, padded_2(): lax.ppermute(head, axis, [((i + 1) % count, i) for i in range(ends)])  40.5 us
    ppermute x10, starting transfers between devices, padded_2(): lax.ppermute(tail, axis, [(i, (i + 1) % count) for i in range(ends)])  33.7 us
    all_to_all x1, blocking collectives, to_particles(): lax.all_to_all(ordered, 'gy', split_axis=2, concat_axis=2, tiled=True)  26.5 us
    all_to_all x1, starting transfers between devices, to_fluid(): lax.all_to_all(fields, 'gx', split_axis=3, concat_axis=2, tiled=True)  18.5 us
    ppermute x10, starting transfers between devices, padded_2(): lax.ppermute(head, axis, [((i + 1) % count, i) for i in range(ends)])  12.9 us
    all_to_all x1, waiting for transfers between devices, to_particles(): lax.all_to_all(lax.all_to_all(ordered, 'gy', split_axis=2, concat_axis=2,...  12.2 us
    unnamed x10, local copies, waits for them, and re-layouts  12.1 us
    all_to_all x1, waiting for transfers between devices, to_fluid(): lax.all_to_all(fields, 'gx', split_axis=3, concat_axis=2, tiled=True)  6.72 us
  transfers between devices with their start and end apart: 23, of which 20 were waited for; matrix products, arithmetic and copies ran while one was open for 5% of the time, Pallas kernels for 0%

commit v1 on v0

--- a/solution.py
+++ b/solution.py
@@ -2,11 +2,21 @@
 import jax.numpy as jnp
 from jax import lax
 from jax.sharding import PartitionSpec as P
+from jax.lax import all_to_all, axis_size
 
 SWEEPS = 8
 particle_volume = 0.05
 time_step = 0.5
 viscosity = 0.1
+lay_the_ranges = lambda obj, peer_axis: jnp.concatenate(
+    all_to_all(
+        jnp.stack(jnp.split(obj, axis_size(peer_axis), axis=3)),
+        split_axis=0,
+        concat_axis=0,
+        axis_name=peer_axis,
+    ),
+    2,
+)
 
 
 def padded_2(cells, sides, width):
@@ -122,11 +132,7 @@
 
 def to_fluid(fields):
     moved = lax.all_to_all(
-        lax.all_to_all(fields, "gx", split_axis=3, concat_axis=2, tiled=True),
-        "gy",
-        split_axis=2,
-        concat_axis=2,
-        tiled=True,
+        lay_the_ranges(fields, "gx"), "gy", split_axis=2, concat_axis=2, tiled=True
     )
     return order_inward(moved, lax.axis_size("gx"), lax.axis_size("gy"))
 

time: 202 us -> 192 us (0.950)
  local copies, waits for them, and re-layouts: 21.6 us -> 10.1 us
  other arithmetic: 9.39 us -> 12.1 us
    unnamed x10 -> x13, local copies, waits for them, and re-layouts: 12.1 us -> 5.01 us
    all_to_all x3 -> x2, local copies, waits for them, and re-layouts: 4.02 us -> 0.07 us  [the longest x1 0.05 us: to_fluid(): lax.all_to_all(lay_the_ranges(fields, 'gx'), 'gy', split_axis=2, concat_a...]
    concatenate x9, other arithmetic: 1.73 us -> 4.76 us  [padded_2(): jnp.concatenate([lax.ppermute(tail, axis, [(i, (i + 1) % count) for i in...]
    broadcast_in_dim x1 -> x0, local copies, waits for them, and re-layouts: 2.66 us -> none  [shards(): pressure_out = to_fluid(pressure[None])[0]]
  transfers between devices with their start and end apart: 23 -> 23, of which waited for: 20 -> 20; matrix products, arithmetic and copies ran while one was open for 5% -> 4% of each run, Pallas kernels for 0% -> 0%
where the time goes in v1:
time: 192 us; the launch traced here: 191 us
  starting transfers between devices  72.6 us (38%)
  waiting for transfers between devices  69.2 us (36%)
  blocking collectives  26.4 us (14%)
  other arithmetic  12.1 us (6%)
  local copies, waits for them, and re-layouts  10.1 us (5%)
    ppermute x10, waiting for transfers between devices, padded_2(): lax.ppermute(head, axis, [((i + 1) % count, i) for i in range(ends)])  40.3 us
    ppermute x10, starting transfers between devices, padded_2(): lax.ppermute(tail, axis, [(i, (i + 1) % count) for i in range(ends)])  32.8 us
    all_to_all x1, blocking collectives, to_particles(): lax.all_to_all(ordered, 'gy', split_axis=2, concat_axis=2, tiled=True)  26.4 us
    all_to_all x1, starting transfers between devices, all_to_all(jnp.stack(jnp.split(obj, axis_size(peer_axis), axis=3)), split...  19.5 us
    ppermute x10, starting transfers between devices, padded_2(): lax.ppermute(head, axis, [((i + 1) % count, i) for i in range(ends)])  13.1 us
    all_to_all x1, waiting for transfers between devices, to_particles(): lax.all_to_all(lax.all_to_all(ordered, 'gy', split_axis=2, concat_axis=2,...  12.5 us
    all_to_all x1, waiting for transfers between devices, to_fluid(): lax.all_to_all(lay_the_ranges(fields, 'gx'), 'gy', split_axis=2, concat_a...  6.95 us
    all_to_all x1, waiting for transfers between devices, all_to_all(jnp.stack(jnp.split(obj, axis_size(peer_axis), axis=3)), split...  6.47 us
  transfers between devices with their start and end apart: 23, of which 20 were waited for; matrix products, arithmetic and copies ran while one was open for 4% of the time, Pallas kernels for 0%

profile of v1, /device:TPU:0, one launch (start us, length us, event | category | flops | bytes accessed | tf_op | source)
XLA Modules:
  0.0 191.4 jit_solution(9085859383611775097)
XLA Ops:
  2.3 26.4 %all_to_all.33 = f32[3,8,64,128]{3,1,0,2:T(8,128)} all-to-all(f32[3,8,64,128]{3,1,0,2:T(8,128)S(1)} %copy.24), channel_id=1, replica_groups=mesh['gx'=8,'gy'=4] {'gy'}, dimensions={2} | all-to-all | bytes 1572864 | tf_op jit(solution)/shard_map/all_to_all | solution.py:143
  28.7 3.7 %all-to-all-start.1 = ((f32[3,8,64,128]{3,1,0,2:T(8,128)}), f32[3,8,64,128]{3,1,0,2:T(8,128)S(1)}, u32[]{:S(2)}, u32[]{:S(2)}) async-start(f32[3,8,64,128]{3,1,0,2:T(8,128)} %all_to_all.33), calls=%async_computation.1 | async-start | bytes 1572864 | tf_op jit(solution)/shard_map/all_to_all | solution.py:142
  32.5 12.5 %all-to-all-done.1 = f32[3,8,64,128]{3,1,0,2:T(8,128)S(1)} async-done(((f32[3,8,64,128]{3,1,0,2:T(8,128)}), f32[3,8,64,128]{3,1,0,2:T(8,128)S(1)}, u32[]{:S(2)}, u32[]{:S(2)}) %all-to-all-start.1) | async-done | bytes 786464 | tf_op jit(solution)/shard_map/all_to_all | solution.py:142
  49.9 4.8 %collective-permute-done.1 = f32[4,8,1,1024]{3,2,1,0:T(1,128)S(1)} collective-permute-done((f32[4,8,1,1024]{3,2,1,0:T(1,128)S(1)}, f32[4,8,1,1024]{3,2,1,0:T(1,128)S(1)}, u32[]{:S(2)}, u32[]{:S(2)}) %collective-permute-start.1) | collective-permute-done | bytes 131104 | tf_op jit(solution)/shard_map/ppermute | solution.py:32
  58.9 2.5 %collective-permute-start.2 = (f32[1,8,1,1024]{3,2,1,0:T(1,128)S(1)}, f32[1,8,1,1024]{3,2,1,0:T(1,128)S(1)}, u32[]{:S(2)}, u32[]{:S(2)}) collective-permute-start(f32[1,8,1,1024]{3,2,1,0:T(1,128)S(1)} %get-tuple-element.11), channel_id=1, source_target_pairs={{0,1},{1,2},{2,3},{3,4},{4,5},{5,6},{6,7},{7,8},{8,9},{9,10},{10,1... | collective-permute-start | bytes 98312 | tf_op jit(solution)/shard_map/ppermute | solution.py:30
  63.1 4.5 %collective-permute-done.3 = f32[1,8,1,1024]{3,2,1,0:T(1,128)S(1)} collective-permute-done((f32[1,8,1,1024]{3,2,1,0:T(1,128)S(1)}, f32[1,8,1,1024]{3,2,1,0:T(1,128)S(1)}, u32[]{:S(2)}, u32[]{:S(2)}) %collective-permute-start.3) | collective-permute-done | bytes 32800 | tf_op jit(solution)/shard_map/ppermute | solution.py:32
  68.6 3.9 %collective-permute-start.4 = (f32[8,1,1024]{2,1,0:T(1,128)S(1)}, f32[8,1,1024]{2,1,0:T(1,128)S(1)}, u32[]{:S(2)}, u32[]{:S(2)}) collective-permute-start(f32[8,1,1024]{2,1,0:T(1,128)S(1)} %get-tuple-element.37), channel_id=1, source_target_pairs={{0,1},{1,2},{2,3},{3,4},{4,5},{5,6},{6,7},{7,8},{8,9},{9,10},{10,1... | collective-permute-start | bytes 98312 | tf_op jit(solution)/shard_map/ppermute | solution.py:30
  74.1 4.2 %collective-permute-done.5 = f32[8,1,1024]{2,1,0:T(1,128)S(1)} collective-permute-done((f32[8,1,1024]{2,1,0:T(1,128)S(1)}, f32[8,1,1024]{2,1,0:T(1,128)S(1)}, u32[]{:S(2)}, u32[]{:S(2)}) %collective-permute-start.5) | collective-permute-done | bytes 32800 | tf_op jit(solution)/shard_map/ppermute | solution.py:32
  83.0 4.2 %collective-permute-done.7 = f32[8,1,1024]{2,1,0:T(1,128)S(1)} collective-permute-done((f32[8,1,1024]{2,1,0:T(1,128)S(1)}, f32[8,1,1024]{2,1,0:T(1,128)S(1)}, u32[]{:S(2)}, u32[]{:S(2)}) %collective-permute-start.7) | collective-permute-done | bytes 32800 | tf_op jit(solution)/shard_map/ppermute | solution.py:32
  88.1 2.9 %collective-permute-start.8 = (f32[8,1,1024]{2,1,0:T(1,128)S(1)}, f32[8,1,1024]{2,1,0:T(1,128)S(1)}, u32[]{:S(2)}, u32[]{:S(2)}) collective-permute-start(f32[8,1,1024]{2,1,0:T(1,128)S(1)} %get-tuple-element.33), channel_id=1, source_target_pairs={{0,1},{1,2},{2,3},{3,4},{4,5},{5,6},{6,7},{7,8},{8,9},{9,10},{10,1... | collective-permute-start | bytes 98312 | tf_op jit(solution)/shard_map/ppermute | solution.py:30
  92.6 4.2 %collective-permute-done.9 = f32[8,1,1024]{2,1,0:T(1,128)S(1)} collective-permute-done((f32[8,1,1024]{2,1,0:T(1,128)S(1)}, f32[8,1,1024]{2,1,0:T(1,128)S(1)}, u32[]{:S(2)}, u32[]{:S(2)}) %collective-permute-start.9) | collective-permute-done | bytes 32800 | tf_op jit(solution)/shard_map/ppermute | solution.py:32
  97.7 4.1 %collective-permute-start.10 = (f32[8,1,1024]{2,1,0:T(1,128)S(1)}, f32[8,1,1024]{2,1,0:T(1,128)S(1)}, u32[]{:S(2)}, u32[]{:S(2)}) collective-permute-start(f32[8,1,1024]{2,1,0:T(1,128)S(1)} %get-tuple-element.31), channel_id=1, source_target_pairs={{0,1},{1,2},{2,3},{3,4},{4,5},{5,6},{6,7},{7,8},{8,9},{9,10},{10,1... | collective-permute-start | bytes 98312 | tf_op jit(solution)/shard_map/ppermute | solution.py:30
  103.4 4.6 %collective-permute-done.11 = f32[8,1,1024]{2,1,0:T(1,128)S(1)} collective-permute-done((f32[8,1,1024]{2,1,0:T(1,128)S(1)}, f32[8,1,1024]{2,1,0:T(1,128)S(1)}, u32[]{:S(2)}, u32[]{:S(2)}) %collective-permute-start.11) | collective-permute-done | bytes 32800 | tf_op jit(solution)/shard_map/ppermute | solution.py:32
  108.9 3.9 %collective-permute-start.12 = (f32[8,1,1024]{2,1,0:T(1,128)S(1)}, f32[8,1,1024]{2,1,0:T(1,128)S(1)}, u32[]{:S(2)}, u32[]{:S(2)}) collective-permute-start(f32[8,1,1024]{2,1,0:T(1,128)S(1)} %get-tuple-element.29), channel_id=1, source_target_pairs={{0,1},{1,2},{2,3},{3,4},{4,5},{5,6},{6,7},{7,8},{8,9},{9,10},{10,1... | collective-permute-start | bytes 98312 | tf_op jit(solution)/shard_map/ppermute | solution.py:30
  114.4 4.6 %collective-permute-done.13 = f32[8,1,1024]{2,1,0:T(1,128)S(1)} collective-permute-done((f32[8,1,1024]{2,1,0:T(1,128)S(1)}, f32[8,1,1024]{2,1,0:T(1,128)S(1)}, u32[]{:S(2)}, u32[]{:S(2)}) %collective-permute-start.13) | collective-permute-done | bytes 32800 | tf_op jit(solution)/shard_map/ppermute | solution.py:32
  119.8 3.7 %collective-permute-start.14 = (f32[8,1,1024]{2,1,0:T(1,128)S(1)}, f32[8,1,1024]{2,1,0:T(1,128)S(1)}, u32[]{:S(2)}, u32[]{:S(2)}) collective-permute-start(f32[8,1,1024]{2,1,0:T(1,128)S(1)} %get-tuple-element.27), channel_id=1, source_target_pairs={{0,1},{1,2},{2,3},{3,4},{4,5},{5,6},{6,7},{7,8},{8,9},{9,10},{10,1... | collective-permute-start | bytes 98312 | tf_op jit(solution)/shard_map/ppermute | solution.py:30
  125.1 4.6 %collective-permute-done.15 = f32[8,1,1024]{2,1,0:T(1,128)S(1)} collective-permute-done((f32[8,1,1024]{2,1,0:T(1,128)S(1)}, f32[8,1,1024]{2,1,0:T(1,128)S(1)}, u32[]{:S(2)}, u32[]{:S(2)}) %collective-permute-start.15) | collective-permute-done | bytes 32800 | tf_op jit(solution)/shard_map/ppermute | solution.py:32
  130.6 3.7 %collective-permute-start.16 = (f32[8,1,1024]{2,1,0:T(1,128)S(1)}, f32[8,1,1024]{2,1,0:T(1,128)S(1)}, u32[]{:S(2)}, u32[]{:S(2)}) collective-permute-start(f32[8,1,1024]{2,1,0:T(1,128)S(1)} %get-tuple-element.25), channel_id=1, source_target_pairs={{0,1},{1,2},{2,3},{3,4},{4,5},{5,6},{6,7},{7,8},{8,9},{9,10},{10,1... | collective-permute-start | bytes 98312 | tf_op jit(solution)/shard_map/ppermute | solution.py:30
  135.9 4.6 %collective-permute-done.17 = f32[8,1,1024]{2,1,0:T(1,128)S(1)} collective-permute-done((f32[8,1,1024]{2,1,0:T(1,128)S(1)}, f32[8,1,1024]{2,1,0:T(1,128)S(1)}, u32[]{:S(2)}, u32[]{:S(2)}) %collective-permute-start.17) | collective-permute-done | bytes 32800 | tf_op jit(solution)/shard_map/ppermute | solution.py:32
  141.3 3.7 %collective-permute-start.19 = (f32[8,1,1024]{2,1,0:T(1,128)S(1)}, f32[8,1,1024]{2,1,0:T(1,128)S(1)}, u32[]{:S(2)}, u32[]{:S(2)}) collective-permute-start(f32[8,1,1024]{2,1,0:T(1,128)S(1)} %get-tuple-element.23), channel_id=1, source_target_pairs={{0,1},{1,2},{2,3},{3,4},{4,5},{5,6},{6,7},{7,8},{8,9},{9,10},{10,1... | collective-permute-start | bytes 98312 | tf_op jit(solution)/shard_map/ppermute | solution.py:30
  151.3 19.5 %all-to-all-start.2 = ((f32[8,1,8,8,128]{4,3,2,1,0:T(8,128)}), f32[8,1,8,8,128]{4,3,2,1,0:T(8,128)S(1)}, u32[]{:S(2)}, u32[]{:S(2)}) async-start(f32[8,1,8,8,128]{4,3,2,1,0:T(8,128)} %fusion.122), calls=%async_computation.2 | async-start | bytes 524288 | tf_op jit(solution)/shard_map/all_to_all | solution.py:12
  171.2 6.5 %all-to-all-done.2 = f32[8,1,8,8,128]{4,3,2,1,0:T(8,128)S(1)} async-done(((f32[8,1,8,8,128]{4,3,2,1,0:T(8,128)}), f32[8,1,8,8,128]{4,3,2,1,0:T(8,128)S(1)}, u32[]{:S(2)}, u32[]{:S(2)}) %all-to-all-start.2) | async-done | bytes 262176 | tf_op jit(solution)/shard_map/all_to_all | solution.py:12
  178.6 3.4 %all-to-all-start.3 = ((f32[1,8,64,128]{3,1,0,2:T(8,128)}), f32[1,8,64,128]{3,1,0,2:T(8,128)S(1)}, u32[]{:S(2)}, u32[]{:S(2)}) async-start(f32[1,8,64,128]{3,1,0,2:T(8,128)} %copy.27), calls=%async_computation.3 | async-start | bytes 524288 | tf_op jit(solution)/shard_map/all_to_all | solution.py:134
  183.6 7.0 %all-to-all-done.3 = f32[1,8,64,128]{3,1,0,2:T(8,128)S(1)} async-done(((f32[1,8,64,128]{3,1,0,2:T(8,128)}), f32[1,8,64,128]{3,1,0,2:T(8,128)S(1)}, u32[]{:S(2)}, u32[]{:S(2)}) %all-to-all-start.3) | async-done | bytes 262176 | tf_op jit(solution)/shard_map/all_to_all | solution.py:134
  (82 shorter events, 42.6 us)
Async XLA Ops:
  1.8 30.6 %copy-start = (f32[8,8,1024]{2,1,0:T(8,128)S(1)}, f32[8,8,1024]{2,1,0:T(8,128)}, u32[]{:S(2)}) copy-start(f32[8,8,1024]{2,1,0:T(8,128)} %param.5) | copy-start | bytes 786436
  28.7 16.3 %all-to-all-start.1 = ((f32[3,8,64,128]{3,1,0,2:T(8,128)}), f32[3,8,64,128]{3,1,0,2:T(8,128)S(1)}, u32[]{:S(2)}, u32[]{:S(2)}) async-start(f32[3,8,64,128]{3,1,0,2:T(8,128)} %all_to_all.33), calls=%async_computation.1 | async-start | bytes 1572864 | tf_op jit(solution)/shard_map/all_to_all | solution.py:142
  45.3 4.6 %collective-permute-start = (f32[4,8,1,1024]{3,2,1,0:T(1,128)S(1)}, f32[4,8,1,1024]{3,2,1,0:T(1,128)S(1)}, u32[]{:S(2)}, u32[]{:S(2)}) collective-permute-start(f32[4,8,1,1024]{3,2,1,0:T(1,128)S(1)} %get-tuple-element.9), channel_id=1, source_target_pairs={{0,1},{1,2},{2,3},{3,4},{4,5},{5,6},{6,7},{7,8},{8,9},{9,10},{10,1... | collective-permute-start | bytes 393224 | tf_op jit(solution)/shard_map/ppermute | solution.py:30
  47.4 7.3 %collective-permute-start.1 = (f32[4,8,1,1024]{3,2,1,0:T(1,128)S(1)}, f32[4,8,1,1024]{3,2,1,0:T(1,128)S(1)}, u32[]{:S(2)}, u32[]{:S(2)}) collective-permute-start(f32[4,8,1,1024]{3,2,1,0:T(1,128)S(1)} %get-tuple-element.10), channel_id=1, source_target_pairs={{1,0},{2,1},{3,2},{4,3},{5,4},{6,5},{7,6},{8,7},{9,8},{10,9},{11,1... | collective-permute-start | bytes 393224 | tf_op jit(solution)/shard_map/ppermute | solution.py:32
  58.9 4.2 %collective-permute-start.2 = (f32[1,8,1,1024]{3,2,1,0:T(1,128)S(1)}, f32[1,8,1,1024]{3,2,1,0:T(1,128)S(1)}, u32[]{:S(2)}, u32[]{:S(2)}) collective-permute-start(f32[1,8,1,1024]{3,2,1,0:T(1,128)S(1)} %get-tuple-element.11), channel_id=1, source_target_pairs={{0,1},{1,2},{2,3},{3,4},{4,5},{5,6},{6,7},{7,8},{8,9},{9,10},{10,1... | collective-permute-start | bytes 98312 | tf_op jit(solution)/shard_map/ppermute | solution.py:30
  61.4 6.3 %collective-permute-start.3 = (f32[1,8,1,1024]{3,2,1,0:T(1,128)S(1)}, f32[1,8,1,1024]{3,2,1,0:T(1,128)S(1)}, u32[]{:S(2)}, u32[]{:S(2)}) collective-permute-start(f32[1,8,1,1024]{3,2,1,0:T(1,128)S(1)} %get-tuple-element.12), channel_id=1, source_target_pairs={{1,0},{2,1},{3,2},{4,3},{5,4},{6,5},{7,6},{8,7},{9,8},{10,9},{11,1... | collective-permute-start | bytes 98312 | tf_op jit(solution)/shard_map/ppermute | solution.py:32
  68.6 5.5 %collective-permute-start.4 = (f32[8,1,1024]{2,1,0:T(1,128)S(1)}, f32[8,1,1024]{2,1,0:T(1,128)S(1)}, u32[]{:S(2)}, u32[]{:S(2)}) collective-permute-start(f32[8,1,1024]{2,1,0:T(1,128)S(1)} %get-tuple-element.37), channel_id=1, source_target_pairs={{0,1},{1,2},{2,3},{3,4},{4,5},{5,6},{6,7},{7,8},{8,9},{9,10},{10,1... | collective-permute-start | bytes 98312 | tf_op jit(solution)/shard_map/ppermute | solution.py:30
  72.5 5.8 %collective-permute-start.5 = (f32[8,1,1024]{2,1,0:T(1,128)S(1)}, f32[8,1,1024]{2,1,0:T(1,128)S(1)}, u32[]{:S(2)}, u32[]{:S(2)}) collective-permute-start(f32[8,1,1024]{2,1,0:T(1,128)S(1)} %get-tuple-element.38), channel_id=1, source_target_pairs={{1,0},{2,1},{3,2},{4,3},{5,4},{6,5},{7,6},{8,7},{9,8},{10,9},{11,1... | collective-permute-start | bytes 98312 | tf_op jit(solution)/shard_map/ppermute | solution.py:32
  79.2 3.8 %collective-permute-start.6 = (f32[8,1,1024]{2,1,0:T(1,128)S(1)}, f32[8,1,1024]{2,1,0:T(1,128)S(1)}, u32[]{:S(2)}, u32[]{:S(2)}) collective-permute-start(f32[8,1,1024]{2,1,0:T(1,128)S(1)} %get-tuple-element.35), channel_id=1, source_target_pairs={{0,1},{1,2},{2,3},{3,4},{4,5},{5,6},{6,7},{7,8},{8,9},{9,10},{10,1... | collective-permute-start | bytes 98312 | tf_op jit(solution)/shard_map/ppermute | solution.py:30
  81.4 5.8 %collective-permute-start.7 = (f32[8,1,1024]{2,1,0:T(1,128)S(1)}, f32[8,1,1024]{2,1,0:T(1,128)S(1)}, u32[]{:S(2)}, u32[]{:S(2)}) collective-permute-start(f32[8,1,1024]{2,1,0:T(1,128)S(1)} %get-tuple-element.36), channel_id=1, source_target_pairs={{1,0},{2,1},{3,2},{4,3},{5,4},{6,5},{7,6},{8,7},{9,8},{10,9},{11,1... | collective-permute-start | bytes 98312 | tf_op jit(solution)/shard_map/ppermute | solution.py:32
  88.1 4.5 %collective-permute-start.8 = (f32[8,1,1024]{2,1,0:T(1,128)S(1)}, f32[8,1,1024]{2,1,0:T(1,128)S(1)}, u32[]{:S(2)}, u32[]{:S(2)}) collective-permute-start(f32[8,1,1024]{2,1,0:T(1,128)S(1)} %get-tuple-element.33), channel_id=1, source_target_pairs={{0,1},{1,2},{2,3},{3,4},{4,5},{5,6},{6,7},{7,8},{8,9},{9,10},{10,1... | collective-permute-start | bytes 98312 | tf_op jit(solution)/shard_map/ppermute | solution.py:30
  91.0 5.8 %collective-permute-start.9 = (f32[8,1,1024]{2,1,0:T(1,128)S(1)}, f32[8,1,1024]{2,1,0:T(1,128)S(1)}, u32[]{:S(2)}, u32[]{:S(2)}) collective-permute-start(f32[8,1,1024]{2,1,0:T(1,128)S(1)} %get-tuple-element.34), channel_id=1, source_target_pairs={{1,0},{2,1},{3,2},{4,3},{5,4},{6,5},{7,6},{8,7},{9,8},{10,9},{11,1... | collective-permute-start | bytes 98312 | tf_op jit(solution)/shard_map/ppermute | solution.py:32
  97.7 5.7 %collective-permute-start.10 = (f32[8,1,1024]{2,1,0:T(1,128)S(1)}, f32[8,1,1024]{2,1,0:T(1,128)S(1)}, u32[]{:S(2)}, u32[]{:S(2)}) collective-permute-start(f32[8,1,1024]{2,1,0:T(1,128)S(1)} %get-tuple-element.31), channel_id=1, source_target_pairs={{0,1},{1,2},{2,3},{3,4},{4,5},{5,6},{6,7},{7,8},{8,9},{9,10},{10,1... | collective-permute-start | bytes 98312 | tf_op jit(solution)/shard_map/ppermute | solution.py:30
  101.8 6.2 %collective-permute-start.11 = (f32[8,1,1024]{2,1,0:T(1,128)S(1)}, f32[8,1,1024]{2,1,0:T(1,128)S(1)}, u32[]{:S(2)}, u32[]{:S(2)}) collective-permute-start(f32[8,1,1024]{2,1,0:T(1,128)S(1)} %get-tuple-element.32), channel_id=1, source_target_pairs={{1,0},{2,1},{3,2},{4,3},{5,4},{6,5},{7,6},{8,7},{9,8},{10,9},{11,1... | collective-permute-start | bytes 98312 | tf_op jit(solution)/shard_map/ppermute | solution.py:32
  108.9 5.5 %collective-permute-start.12 = (f32[8,1,1024]{2,1,0:T(1,128)S(1)}, f32[8,1,1024]{2,1,0:T(1,128)S(1)}, u32[]{:S(2)}, u32[]{:S(2)}) collective-permute-start(f32[8,1,1024]{2,1,0:T(1,128)S(1)} %get-tuple-element.29), channel_id=1, source_target_pairs={{0,1},{1,2},{2,3},{3,4},{4,5},{5,6},{6,7},{7,8},{8,9},{9,10},{10,1... | collective-permute-start | bytes 98312 | tf_op jit(solution)/shard_map/ppermute | solution.py:30
  112.8 6.1 %collective-permute-start.13 = (f32[8,1,1024]{2,1,0:T(1,128)S(1)}, f32[8,1,1024]{2,1,0:T(1,128)S(1)}, u32[]{:S(2)}, u32[]{:S(2)}) collective-permute-start(f32[8,1,1024]{2,1,0:T(1,128)S(1)} %get-tuple-element.30), channel_id=1, source_target_pairs={{1,0},{2,1},{3,2},{4,3},{5,4},{6,5},{7,6},{8,7},{9,8},{10,9},{11,1... | collective-permute-start | bytes 98312 | tf_op jit(solution)/shard_map/ppermute | solution.py:32
  119.8 5.3 %collective-permute-start.14 = (f32[8,1,1024]{2,1,0:T(1,128)S(1)}, f32[8,1,1024]{2,1,0:T(1,128)S(1)}, u32[]{:S(2)}, u32[]{:S(2)}) collective-permute-start(f32[8,1,1024]{2,1,0:T(1,128)S(1)} %get-tuple-element.27), channel_id=1, source_target_pairs={{0,1},{1,2},{2,3},{3,4},{4,5},{5,6},{6,7},{7,8},{8,9},{9,10},{10,1... | collective-permute-start | bytes 98312 | tf_op jit(solution)/shard_map/ppermute | solution.py:30
  123.6 6.1 %collective-permute-start.15 = (f32[8,1,1024]{2,1,0:T(1,128)S(1)}, f32[8,1,1024]{2,1,0:T(1,128)S(1)}, u32[]{:S(2)}, u32[]{:S(2)}) collective-permute-start(f32[8,1,1024]{2,1,0:T(1,128)S(1)} %get-tuple-element.28), channel_id=1, source_target_pairs={{1,0},{2,1},{3,2},{4,3},{5,4},{6,5},{7,6},{8,7},{9,8},{10,9},{11,1... | collective-permute-start | bytes 98312 | tf_op jit(solution)/shard_map/ppermute | solution.py:32
  130.6 5.3 %collective-permute-start.16 = (f32[8,1,1024]{2,1,0:T(1,128)S(1)}, f32[8,1,1024]{2,1,0:T(1,128)S(1)}, u32[]{:S(2)}, u32[]{:S(2)}) collective-permute-start(f32[8,1,1024]{2,1,0:T(1,128)S(1)} %get-tuple-element.25), channel_id=1, source_target_pairs={{0,1},{1,2},{2,3},{3,4},{4,5},{5,6},{6,7},{7,8},{8,9},{9,10},{10,1... | collective-permute-start | bytes 98312 | tf_op jit(solution)/shard_map/ppermute | solution.py:30
  134.3 6.1 %collective-permute-start.17 = (f32[8,1,1024]{2,1,0:T(1,128)S(1)}, f32[8,1,1024]{2,1,0:T(1,128)S(1)}, u32[]{:S(2)}, u32[]{:S(2)}) collective-permute-start(f32[8,1,1024]{2,1,0:T(1,128)S(1)} %get-tuple-element.26), channel_id=1, source_target_pairs={{1,0},{2,1},{3,2},{4,3},{5,4},{6,5},{7,6},{8,7},{9,8},{10,9},{11,1... | collective-permute-start | bytes 98312 | tf_op jit(solution)/shard_map/ppermute | solution.py:32
  141.3 29.5 %collective-permute-start.19 = (f32[8,1,1024]{2,1,0:T(1,128)S(1)}, f32[8,1,1024]{2,1,0:T(1,128)S(1)}, u32[]{:S(2)}, u32[]{:S(2)}) collective-permute-start(f32[8,1,1024]{2,1,0:T(1,128)S(1)} %get-tuple-element.23), channel_id=1, source_target_pairs={{0,1},{1,2},{2,3},{3,4},{4,5},{5,6},{6,7},{7,8},{8,9},{9,10},{10,1... | collective-permute-start | bytes 98312 | tf_op jit(solution)/shard_map/ppermute | solution.py:30
  145.0 25.8 %collective-permute-start.18 = (f32[8,1,1024]{2,1,0:T(1,128)S(1)}, f32[8,1,1024]{2,1,0:T(1,128)S(1)}, u32[]{:S(2)}, u32[]{:S(2)}) collective-permute-start(f32[8,1,1024]{2,1,0:T(1,128)S(1)} %get-tuple-element.24), channel_id=1, source_target_pairs={{1,0},{2,1},{3,2},{4,3},{5,4},{6,5},{7,6},{8,7},{9,8},{10,9},{11,1... | collective-permute-start | bytes 98312 | tf_op jit(solution)/shard_map/ppermute | solution.py:32
  151.3 26.4 %all-to-all-start.2 = ((f32[8,1,8,8,128]{4,3,2,1,0:T(8,128)}), f32[8,1,8,8,128]{4,3,2,1,0:T(8,128)S(1)}, u32[]{:S(2)}, u32[]{:S(2)}) async-start(f32[8,1,8,8,128]{4,3,2,1,0:T(8,128)} %fusion.122), calls=%async_computation.2 | async-start | bytes 524288 | tf_op jit(solution)/shard_map/all_to_all | solution.py:12
  178.6 12.0 %all-to-all-start.3 = ((f32[1,8,64,128]{3,1,0,2:T(8,128)}), f32[1,8,64,128]{3,1,0,2:T(8,128)S(1)}, u32[]{:S(2)}, u32[]{:S(2)}) async-start(f32[1,8,64,128]{3,1,0,2:T(8,128)} %copy.27), calls=%async_computation.3 | async-start | bytes 524288 | tf_op jit(solution)/shard_map/all_to_all | solution.py:134
  (2 other events, 31.7 us)
